TPU v7x, 128 devices: a whole 4x4x4 slice. The times are simulated.
128 devices in a mesh: grp: 16 (over y, z_lo, core), tile: 8 (over z_hi, x).
Axes of the slice: x: 4, y: 4, z: 4 (z_hi: 2, z_lo: 2; z = z_hi * 2 + z_lo), core: 2. Of those that a mesh axis runs over, the one named last changes fastest.
Arguments:
- parent_so2: float32 [4, 1024, 1024], P(None, 'grp', 'tile'), may hold values from 0.1 to 10
- wind_east: float32 [4, 1024, 1024], P(None, 'grp', 'tile'), may hold values from -0.2 to 0.2
- wind_north: float32 [4, 1024, 1024], P(None, 'grp', 'tile'), may hold values from -0.2 to 0.2
- diffusivity: float32 [4, 1024, 1024], P(None, 'grp', 'tile'), may hold values from 0.01 to 0.25
- nest_so2: float32 [16, 4, 320, 320], P('grp', None, 'tile'), may hold values from 0.1 to 10
- nest_rows: int32 [16], replicated, may hold values from 0 to 15, as said below
- nest_offset: int32 [16], replicated, may hold values from 1 to 31
- nest_left: int32 [16], replicated, may hold values from 1 to 991
- nest_height: int32 [16], replicated, may hold values from 16 to 32
- nest_width: int32 [16], replicated, may hold values from 16 to 32
Outputs:
- parent_next: float32 [4, 1024, 1024], P(None, 'grp', 'tile')
- nest_next: float32 [16, 4, 320, 320], P('grp', None, 'tile')
Inputs may be any that keep to these rules, and one draw needn't show every extreme that they name: `nest_rows`: each of 0 to 15 appears once.
All inputs are finite; a program needn't handle non-finite values.
Results may differ from a plain program's by a relative error of at most 0.0001.
Values sent between devices are 32-bit elements; how exact they have to be, the bound alone decides.
No kernel may reach another device: no remote copies, remote signals or barrier semaphores. Data moves between devices by JAX's collectives and lax.ppermute only.
A program may use at most 64 MiB of HBM per device.

v0:
```python
import jax
import jax.numpy as jnp
from jax import lax
from jax.sharding import PartitionSpec as P

RATIO = 10
FRX = 32
FRY = 32


mixing_rate = 0.02


def extended(x, sides, width):
    for axis, dim in sides:
        devices, length = (lax.axis_size(axis), x.shape[dim])
        up = [(i, (i + 1) % devices) for i in range(devices - 1)]
        down = [(j, i) for i, j in up]
        last = lax.slice_in_dim(x, length - width, length, axis=dim)
        leading = lax.slice_in_dim(x, 0, width, axis=dim)
        before = lax.ppermute(last, axis, up)
        after = lax.ppermute(leading, axis, down)
        x = jnp.concatenate([before, x, after], axis=dim)
    return x


def advance(padded_c, padded_u, padded_v, vertical):
    centre = padded_c[:, 1:-1, 1:-1]
    face_u = 0.5 * (padded_u[:, :-1, 1:-1] + padded_u[:, 1:, 1:-1])
    flux_x = (
        jnp.maximum(face_u, 0.0) * padded_c[:, :-1, 1:-1]
        + jnp.minimum(face_u, 0.0) * padded_c[:, 1:, 1:-1]
    )
    face_v = 0.5 * (padded_v[:, 1:-1, :-1] + padded_v[:, 1:-1, 1:])
    flux_y = (
        jnp.maximum(face_v, 0.0) * padded_c[:, 1:-1, :-1]
        + jnp.minimum(face_v, 0.0) * padded_c[:, 1:-1, 1:]
    )
    spread = (
        padded_c[:, :-2, 1:-1]
        + padded_c[:, 2:, 1:-1]
        + padded_c[:, 1:-1, :-2]
        + padded_c[:, 1:-1, 2:]
        - 4.0 * centre
    )
    coupling = 0.5 * (vertical[:-1] + vertical[1:])
    between = coupling * (centre[1:] - centre[:-1])
    zero_layer = jnp.zeros_like(centre[:1])
    column = jnp.concatenate([between, zero_layer], 0) - jnp.concatenate([zero_layer, between], 0)
    return (
        centre
        - (flux_x[:, 1:] - flux_x[:, :-1])
        - (flux_y[:, :, 1:] - flux_y[:, :, :-1])
        + mixing_rate * spread
        + column
    )


def shards(
    parent_so2,
    wind_east,
    wind_north,
    diffusivity,
    nest_so2,
    nest_rows,
    nest_offset,
    nest_left,
    nest_height,
    nest_width,
):
    level_count, row_count, col_count = parent_so2.shape
    tiles = lax.axis_size("tile")
    group_index = lax.axis_index("grp")
    tile_index = lax.axis_index("tile")
    nest_ids = jnp.arange(nest_rows.shape[0], dtype=jnp.int32)
    mine = nest_ids == group_index
    host_row = jnp.sum(jnp.where(mine, nest_rows, 0))
    host_offset = jnp.sum(jnp.where(mine, nest_offset, 0))
    host_left = jnp.sum(jnp.where(mine, nest_left, 0))
    host_height = jnp.sum(jnp.where(mine, nest_height, 0))
    host_width = jnp.sum(jnp.where(mine, nest_width, 0))
    is_host = nest_rows == group_index
    local_nest = jnp.sum(jnp.where(is_host, nest_ids, 0))
    local_offset = jnp.sum(jnp.where(is_host, nest_offset, 0))
    local_left = jnp.sum(jnp.where(is_host, nest_left, 0))
    local_height = jnp.sum(jnp.where(is_host, nest_height, 0))
    local_width = jnp.sum(jnp.where(is_host, nest_width, 0))
    stacked = jnp.stack([parent_so2, wind_east, wind_north])
    padded = extended(stacked, (("grp", 2), ("tile", 3)), 1)
    stepped = advance(padded[0], padded[1], padded[2], diffusivity)
    fields = jnp.stack([parent_so2, wind_east, wind_north, diffusivity])
    window_top = host_row * row_count + host_offset - 1
    portion = lax.all_gather(fields, "grp", axis=2, tiled=True)
    wanted = window_top + jnp.arange(FRX + 2, dtype=jnp.int32)[:, None]
    offered = jnp.arange(portion.shape[2], dtype=jnp.int32)[None, :]
    selector = (wanted == offered).astype(jnp.float32)
    row_window = jnp.einsum("ip,flpc->flic", selector, portion, precision=lax.Precision.HIGHEST)
    portion = lax.all_gather(row_window, "tile", axis=3, tiled=True)
    offered = jnp.arange(portion.shape[3], dtype=jnp.int32)[:, None]
    wanted = host_left - 1 + jnp.arange(FRY + 2, dtype=jnp.int32)[None, :]
    selector = (offered == wanted).astype(jnp.float32)
    window = jnp.einsum("flrp,pq->flrq", portion, selector, precision=lax.Precision.HIGHEST)
    wide = jnp.concatenate(
        [window[..., :1], jnp.repeat(window[..., 1:-1], RATIO, axis=3), window[..., -1:]], 3
    )
    fine_rows = nest_so2.shape[2]
    fine_cols = nest_so2.shape[3]
    total_rows = fine_rows * tiles
    first_row = tile_index * fine_rows
    col_active = jnp.arange(fine_cols, dtype=jnp.int32) < host_width * RATIO

    def boundary(first, count):
        global_rows = first + jnp.arange(count, dtype=jnp.int32)
        picks = jnp.clip((global_rows + RATIO) // RATIO, 0, FRX + 1)
        return (jnp.take(wide, picks, axis=2), global_rows)

    own_bound, own_rows = boundary(first_row, fine_rows)
    own_active = ((own_rows >= 0) & (own_rows < host_height * RATIO))[:, None] & col_active[None, :]
    start_inner = jnp.where(own_active, nest_so2[0], own_bound[0][:, :, 1:-1])
    field_rows = jnp.concatenate([own_bound[0][:, :, :1], start_inner, own_bound[0][:, :, -1:]], 2)
    ext_bound, ext_rows = boundary(first_row - 1, fine_rows + 2)
    in_domain = ((ext_rows >= 0) & (ext_rows < total_rows))[:, None]
    fine_k = 0.1 * ext_bound[3][:, 1:-1, 1:-1]

    def substep(step_index, current):
        framed = extended(current, (("tile", 1),), 1)
        framed = jnp.where(in_domain, framed, ext_bound[0])
        interior = advance(framed, ext_bound[1], ext_bound[2], fine_k)
        return current.at[:, :, 1:-1].set(jnp.where(own_active, interior, current[:, :, 1:-1]))

    field_rows = lax.fori_loop(0, RATIO, substep, field_rows)
    nest_result = field_rows[:, :, 1:-1]
    coarse_band = jnp.mean(
        nest_result.reshape(level_count, fine_rows // RATIO, RATIO, FRY, RATIO), axis=(2, 4)
    )
    portion = lax.all_gather(coarse_band[None], ("grp", "tile"), axis=0, tiled=True)
    offered = jnp.arange(portion.shape[0], dtype=jnp.int32)
    weights = (offered // tiles == local_nest).astype(jnp.float32)
    places = ((offered % tiles)[:, None] == jnp.arange(tiles, dtype=jnp.int32)[None, :]).astype(
        jnp.float32
    )
    returned = jnp.einsum(
        "k,kt,klrc->ltrc", weights, places, portion, precision=lax.Precision.HIGHEST
    )
    returned = returned.reshape(level_count, FRX, FRY)
    band_rows = jnp.arange(FRX, dtype=jnp.int32)
    band_cols = jnp.arange(FRY, dtype=jnp.int32)
    row_select = (
        (jnp.arange(row_count, dtype=jnp.int32)[:, None] == local_offset + band_rows[None, :])
        & (band_rows[None, :] < local_height)
    ).astype(jnp.float32)
    my_cols = tile_index * col_count + jnp.arange(col_count, dtype=jnp.int32)
    col_select = (
        (my_cols[:, None] == local_left + band_cols[None, :]) & (band_cols[None, :] < local_width)
    ).astype(jnp.float32)
    placed = jnp.einsum(
        "ra,lab,cb->lrc", row_select, returned, col_select, precision=lax.Precision.HIGHEST
    )
    covered = jnp.sum(row_select, 1)[:, None] * jnp.sum(col_select, 1)[None, :] > 0.5
    parent_next = jnp.where(covered, placed, stepped)
    return (parent_next, nest_result[None])


def solution(mesh):
    in_specs = (
        P(None, "grp", "tile"),
        P(None, "grp", "tile"),
        P(None, "grp", "tile"),
        P(None, "grp", "tile"),
        P("grp", None, "tile", None),
        P(),
        P(),
        P(),
        P(),
        P(),
    )
    out_specs = (P(None, "grp", "tile"), P("grp", None, "tile", None))
    return jax.shard_map(shards, mesh=mesh, in_specs=in_specs, out_specs=out_specs, check_vma=False)
```

profile of v0, /device:TPU:0, one launch (start us, length us, event | category | flops | bytes accessed | tf_op | source)
XLA Modules:
  0.0 617.0 jit_solution(16693726348077435953)
XLA Ops:
  7.2 2.0 pad_maximum_fusion.2
  10.1 1.3 collective-permute-start.3
  11.4 3.0 collective-permute-start.2
  14.4 1.5 select_reduce_fusion.6
  19.0 45.3 %all-gather.4.cloned.1.call-done = f32[4,4,1024,128]{3,2,1,0:T(8,128)} async-done(((f32[4,4,64,128]{3,2,1,0:T(8,128)}), f32[4,4,1024,128]{3,2,1,0:T(8,128)}) %all-gather.4.cloned.1.call-update) | async-done | bytes 8388624 | tf_op jit(solution)/shard_map/all_gather | solution.py:93
  64.3 7.4 %convolution_bitcast_fusion = f32[4,4,34,128]{3,2,1,0:T(8,128)} fusion(f32[4,4,1024,128]{3,2,1,0:T(8,128)} %all-gather.4.cloned.1.call-done, s32[34]{0:T(128)S(1)} %iota_add_fusion.1), kind=kOutput, calls=%fused_computation.27 | convolution fusion | flops 855672832 | bytes 8667272 | tf_op jit(solution)/shard_map/ip,flpc->flic/dot_general | solution.py:97
  77.8 1.3 collective-permute-start.5
  79.1 4.8 collective-permute-start.4
  83.9 1.2 compare_convert_fusion
  85.1 10.5 %collective-permute-done.5 = f32[3,4,66,1]{3,2,1,0:T(8,128)S(1)} collective-permute-done((f32[3,4,66,1]{3,2,1,0:T(8,128)S(1)}, f32[3,4,66,1]{3,2,1,0:T(8,128)S(1)}, u32[]{:S(2)}, u32[]{:S(2)}) %collective-permute-start.5) | collective-permute-done | bytes 3200 | tf_op jit(solution)/shard_map/ppermute | solution.py:22
  95.6 1.0 collective-permute-done.4
  98.0 0.9 fusion.22
  98.9 0.9 fusion.15
  99.8 41.0 %all-gather.6.cloned.1.call-done = f32[4,4,34,1024]{3,2,1,0:T(8,128)} async-done(((f32[4,4,34,128]{3,2,1,0:T(8,128)}), f32[4,4,34,1024]{3,2,1,0:T(8,128)}) %all-gather.6.cloned.1.call-update) | async-done | bytes 2228240 | tf_op jit(solution)/shard_map/all_gather | solution.py:98
  140.8 4.5 fusion.20
  146.1 2.6 copy.29
  148.9 1.8 pad_maximum_fusion.1
  150.7 1.2 gather_fusion.1
  153.5 1.3 gather_fusion
  154.8 0.9 select_bitcast_fusion.1
  157.3 119.7 %while.14 = (s32[]{:T(128)}, f32[4,40,322]{2,1,0:T(8,128)S(1)}, f32[4,4,42,322]{3,2,1,0:T(8,128)S(1)}, f32[4,41,320]{2,1,0:T(8,128)S(1)}, f32[4,40,321]{2,1,0:T(...) while((s32[]{:T(128)}, f32[4,40,322]{2,1,0:T(8,128)S(1)}, ...), condition=%wide.region_13.14_spmd.clone, body=%wide.region_12.13_spmd.clone.sunk | while | flops 1630298 | bytes 5829057 | solution.py:131
  157.4 1.3 collective-permute-start
  158.7 4.5 collective-permute-start.1
  163.3 1.2 collective-permute-done.1
  165.7 1.1 scatter.7
  166.9 1.3 collective-permute-start
  168.2 4.8 collective-permute-start.1
  173.1 1.2 collective-permute-done.1
  175.4 1.1 scatter.7
  176.6 1.3 collective-permute-start
  177.9 4.8 collective-permute-start.1
  182.9 1.2 collective-permute-done.1
  185.2 1.1 scatter.7
  186.4 1.3 collective-permute-start
  187.7 5.4 collective-permute-start.1
  193.2 1.2 collective-permute-done.1
  195.6 1.1 scatter.7
  196.8 1.3 collective-permute-start
  198.1 8.4 %collective-permute-start.1 = (f32[4,1,322]{2,1,0:T(1,128)S(1)}, f32[4,1,322]{2,1,0:T(1,128)S(1)}, u32[]{:S(2)}, u32[]{:S(2)}) collective-permute-start(f32[4,1,322]{2,1,0:T(1,128)S(1)} %get-tuple-element.252), channel_id=1, source_target_pairs={{0,1},{1,2},{2,3},{3,4},{4,5},{5,6},{6,7},{8,9},{9,10},{10,11},{11... | collective-permute-start | bytes 15464 | tf_op jit(solution)/shard_map/while/body/eval_jaxpr/ppermute | solution.py:21
  206.6 1.2 collective-permute-done.1
  209.0 1.1 scatter.7
  210.1 1.3 collective-permute-start
  211.4 8.4 %collective-permute-start.1 = (f32[4,1,322]{2,1,0:T(1,128)S(1)}, f32[4,1,322]{2,1,0:T(1,128)S(1)}, u32[]{:S(2)}, u32[]{:S(2)}) collective-permute-start(f32[4,1,322]{2,1,0:T(1,128)S(1)} %get-tuple-element.252), channel_id=1, source_target_pairs={{0,1},{1,2},{2,3},{3,4},{4,5},{5,6},{6,7},{8,9},{9,10},{10,11},{11... | collective-permute-start | bytes 15464 | tf_op jit(solution)/shard_map/while/body/eval_jaxpr/ppermute | solution.py:21
  220.0 1.2 collective-permute-done.1
  222.3 1.1 scatter.7
  223.5 1.3 collective-permute-start
  224.8 8.4 %collective-permute-start.1 = (f32[4,1,322]{2,1,0:T(1,128)S(1)}, f32[4,1,322]{2,1,0:T(1,128)S(1)}, u32[]{:S(2)}, u32[]{:S(2)}) collective-permute-start(f32[4,1,322]{2,1,0:T(1,128)S(1)} %get-tuple-element.252), channel_id=1, source_target_pairs={{0,1},{1,2},{2,3},{3,4},{4,5},{5,6},{6,7},{8,9},{9,10},{10,11},{11... | collective-permute-start | bytes 15464 | tf_op jit(solution)/shard_map/while/body/eval_jaxpr/ppermute | solution.py:21
  233.4 1.2 collective-permute-done.1
  235.7 1.1 scatter.7
  236.9 1.3 collective-permute-start
  238.2 8.4 %collective-permute-start.1 = (f32[4,1,322]{2,1,0:T(1,128)S(1)}, f32[4,1,322]{2,1,0:T(1,128)S(1)}, u32[]{:S(2)}, u32[]{:S(2)}) collective-permute-start(f32[4,1,322]{2,1,0:T(1,128)S(1)} %get-tuple-element.252), channel_id=1, source_target_pairs={{0,1},{1,2},{2,3},{3,4},{4,5},{5,6},{6,7},{8,9},{9,10},{10,11},{11... | collective-permute-start | bytes 15464 | tf_op jit(solution)/shard_map/while/body/eval_jaxpr/ppermute | solution.py:21
  246.7 1.2 collective-permute-done.1
  249.1 1.1 scatter.7
  250.3 1.3 collective-permute-start
  251.6 8.4 %collective-permute-start.1 = (f32[4,1,322]{2,1,0:T(1,128)S(1)}, f32[4,1,322]{2,1,0:T(1,128)S(1)}, u32[]{:S(2)}, u32[]{:S(2)}) collective-permute-start(f32[4,1,322]{2,1,0:T(1,128)S(1)} %get-tuple-element.252), channel_id=1, source_target_pairs={{0,1},{1,2},{2,3},{3,4},{4,5},{5,6},{6,7},{8,9},{9,10},{10,11},{11... | collective-permute-start | bytes 15464 | tf_op jit(solution)/shard_map/while/body/eval_jaxpr/ppermute | solution.py:21
  260.1 1.2 collective-permute-done.1
  262.5 1.1 scatter.7
  263.7 1.3 collective-permute-start
  265.0 8.4 %collective-permute-start.1 = (f32[4,1,322]{2,1,0:T(1,128)S(1)}, f32[4,1,322]{2,1,0:T(1,128)S(1)}, u32[]{:S(2)}, u32[]{:S(2)}) collective-permute-start(f32[4,1,322]{2,1,0:T(1,128)S(1)} %get-tuple-element.252), channel_id=1, source_target_pairs={{0,1},{1,2},{2,3},{3,4},{4,5},{5,6},{6,7},{8,9},{9,10},{10,11},{11... | collective-permute-start | bytes 15464 | tf_op jit(solution)/shard_map/while/body/eval_jaxpr/ppermute | solution.py:21
  273.5 1.2 collective-permute-done.1
  275.8 1.1 scatter.7
  277.8 2.9 reshape.227
  281.1 326.7 %all-gather = f32[512,4,32]{2,1,0:T(4,128)S(1)} all-gather(f32[4,4,32]{2,1,0:T(4,128)S(1)} %broadcast_multiply_fusion), channel_id=2, replica_groups=mesh['grp'=16,'tile'=8] {'grp','tile'}, dimensions={0}, use_global_device_ids=true | all-gather | bytes 264192 | tf_op jit(solution)/shard_map/all_gather | solution.py:136
  609.1 1.1 convolution_select_fusion
  (201 shorter events, 26.5 us)
Async XLA Ops:
  7.2 57.2 %all-gather.4.cloned.1.call-start = ((), (), s32[]{:S(2)}) async-start(), calls=%async_computation | async-start | bytes 8912896 | tf_op jit(solution)/shard_map/all_gather | solution.py:93
  9.2 131.6 %all-gather.6.cloned.1.call-start = ((), (), s32[]{:S(2)}) async-start(), calls=%async_computation.1 | async-start | bytes 2949120 | tf_op jit(solution)/shard_map/all_gather | solution.py:98
  10.1 67.5 %collective-permute-start.3 = (f32[3,4,1,128]{3,2,1,0:T(1,128)S(1)}, f32[3,4,1,128]{3,2,1,0:T(1,128)S(1)}, u32[]{:S(2)}, u32[]{:S(2)}) collective-permute-start(f32[3,4,1,128]{3,2,1,0:T(1,128)S(1)} %get-tuple-element.186), channel_id=1, source_target_pairs={{8,0},{16,8},{24,16},{32,24},{40,32},{48,40},{56,48},{64,56},{72,6... | collective-permute-start | bytes 18440 | tf_op jit(solution)/shard_map/ppermute | solution.py:22
  11.4 66.2 %collective-permute-start.2 = (f32[3,4,1,128]{3,2,1,0:T(1,128)S(1)}, f32[3,4,1,128]{3,2,1,0:T(1,128)S(1)}, u32[]{:S(2)}, u32[]{:S(2)}) collective-permute-start(f32[3,4,1,128]{3,2,1,0:T(1,128)S(1)} %get-tuple-element.185), channel_id=1, source_target_pairs={{0,8},{8,16},{16,24},{24,32},{32,40},{40,48},{48,56},{56,64},{64,7... | collective-permute-start | bytes 18440 | tf_op jit(solution)/shard_map/ppermute | solution.py:21
  19.0 58.6 %copy-start.1 = (f32[4,64,128]{2,1,0:T(8,128)S(1)}, f32[4,64,128]{2,1,0:T(8,128)}, u32[]{:S(2)}) copy-start(f32[4,64,128]{2,1,0:T(8,128)} %param.16) | copy-start | bytes 393220
  19.0 58.6 %copy-start.2 = (f32[4,64,128]{2,1,0:T(8,128)S(1)}, f32[4,64,128]{2,1,0:T(8,128)}, u32[]{:S(2)}) copy-start(f32[4,64,128]{2,1,0:T(8,128)} %param.15) | copy-start | bytes 393220
  19.0 58.6 %copy-start.3 = (f32[4,64,128]{2,1,0:T(8,128)S(1)}, f32[4,64,128]{2,1,0:T(8,128)}, u32[]{:S(2)}) copy-start(f32[4,64,128]{2,1,0:T(8,128)} %param.14) | copy-start | bytes 393220
  72.8 24.3 %copy-start.11 = (pred[40]{0:T(512)(128)(4,1)}, pred[40]{0:T(512)(128)(4,1)S(1)}, u32[]{:S(2)}) copy-start(pred[40]{0:T(512)(128)(4,1)S(1)} %compare_and_fusion.3) | copy-start | bytes 124
  73.4 2.6 copy-start.16
  74.0 23.2 %copy-start.18 = (pred[32]{0:T(512)(128)(4,1)}, pred[32]{0:T(512)(128)(4,1)S(1)}, u32[]{:S(2)}) copy-start(pred[32]{0:T(512)(128)(4,1)S(1)} %iota_compare_fusion.8) | copy-start | bytes 100
  74.0 23.2 %copy-start.20 = (s32[128]{0:T(128)}, s32[128]{0:T(128)S(1)}, u32[]{:S(2)}) copy-start(s32[128]{0:T(128)S(1)} %iota_add_fusion.4) | copy-start | bytes 1540
  74.7 22.5 %copy-start.22 = (s32[32]{0:T(128)}, s32[32]{0:T(128)S(1)}, u32[]{:S(2)}) copy-start(s32[32]{0:T(128)S(1)} %iota_add_fusion.3) | copy-start | bytes 388
  75.4 21.8 %copy-start.24 = (pred[32]{0:T(512)(128)(4,1)}, pred[32]{0:T(512)(128)(4,1)S(1)}, u32[]{:S(2)}) copy-start(pred[32]{0:T(512)(128)(4,1)S(1)} %iota_compare_fusion.7) | copy-start | bytes 100
  77.6 19.6 %copy-start.5 = (f32[4,64,128]{2,1,0:T(8,128)S(1)}, f32[4,64,128]{2,1,0:T(8,128)}, u32[]{:S(2)}) copy-start(f32[4,64,128]{2,1,0:T(8,128)} %param.17) | copy-start | bytes 393220
  77.8 17.7 %collective-permute-start.5 = (f32[3,4,66,1]{3,2,1,0:T(8,128)S(1)}, f32[3,4,66,1]{3,2,1,0:T(8,128)S(1)}, u32[]{:S(2)}, u32[]{:S(2)}) collective-permute-start(f32[3,4,66,1]{3,2,1,0:T(8,128)S(1)} %get-tuple-element.184), channel_id=1, source_target_pairs={{1,0},{2,1},{3,2},{4,3},{5,4},{6,5},{7,6},{9,8},{10,9},{11,10},{12... | collective-permute-start | bytes 9512 | tf_op jit(solution)/shard_map/ppermute | solution.py:22
  79.1 17.5 %collective-permute-start.4 = (f32[3,4,66,1]{3,2,1,0:T(8,128)S(1)}, f32[3,4,66,1]{3,2,1,0:T(8,128)S(1)}, u32[]{:S(2)}, u32[]{:S(2)}) collective-permute-start(f32[3,4,66,1]{3,2,1,0:T(8,128)S(1)} %get-tuple-element.183), channel_id=1, source_target_pairs={{0,1},{1,2},{2,3},{3,4},{4,5},{5,6},{6,7},{8,9},{9,10},{10,11},{11... | collective-permute-start | bytes 9512 | tf_op jit(solution)/shard_map/ppermute | solution.py:21
  154.8 1.1 copy-start.7
  154.8 1.1 copy-start.10
  154.8 2.0 copy-start
  155.8 1.2 copy-start.4
  156.1 1.2 copy-start.12
  157.4 6.0 collective-permute-start
  158.7 5.9 collective-permute-start.1
  166.9 6.2 %collective-permute-start = (f32[4,1,322]{2,1,0:T(1,128)S(1)}, f32[4,1,322]{2,1,0:T(1,128)S(1)}, u32[]{:S(2)}, u32[]{:S(2)}) collective-permute-start(f32[4,1,322]{2,1,0:T(1,128)S(1)} %get-tuple-element.251), channel_id=1, source_target_pairs={{1,0},{2,1},{3,2},{4,3},{5,4},{6,5},{7,6},{9,8},{10,9},{11,10},{12... | collective-permute-start | bytes 15464 | tf_op jit(solution)/shard_map/while/body/eval_jaxpr/ppermute | solution.py:22
  168.2 6.2 collective-permute-start.1
  176.6 6.2 %collective-permute-start = (f32[4,1,322]{2,1,0:T(1,128)S(1)}, f32[4,1,322]{2,1,0:T(1,128)S(1)}, u32[]{:S(2)}, u32[]{:S(2)}) collective-permute-start(f32[4,1,322]{2,1,0:T(1,128)S(1)} %get-tuple-element.251), channel_id=1, source_target_pairs={{1,0},{2,1},{3,2},{4,3},{5,4},{6,5},{7,6},{9,8},{10,9},{11,10},{12... | collective-permute-start | bytes 15464 | tf_op jit(solution)/shard_map/while/body/eval_jaxpr/ppermute | solution.py:22
  177.9 6.2 collective-permute-start.1
  186.4 6.8 %collective-permute-start = (f32[4,1,322]{2,1,0:T(1,128)S(1)}, f32[4,1,322]{2,1,0:T(1,128)S(1)}, u32[]{:S(2)}, u32[]{:S(2)}) collective-permute-start(f32[4,1,322]{2,1,0:T(1,128)S(1)} %get-tuple-element.251), channel_id=1, source_target_pairs={{1,0},{2,1},{3,2},{4,3},{5,4},{6,5},{7,6},{9,8},{10,9},{11,10},{12... | collective-permute-start | bytes 15464 | tf_op jit(solution)/shard_map/while/body/eval_jaxpr/ppermute | solution.py:22
  187.7 6.8 %collective-permute-start.1 = (f32[4,1,322]{2,1,0:T(1,128)S(1)}, f32[4,1,322]{2,1,0:T(1,128)S(1)}, u32[]{:S(2)}, u32[]{:S(2)}) collective-permute-start(f32[4,1,322]{2,1,0:T(1,128)S(1)} %get-tuple-element.252), channel_id=1, source_target_pairs={{0,1},{1,2},{2,3},{3,4},{4,5},{5,6},{6,7},{8,9},{9,10},{10,11},{11... | collective-permute-start | bytes 15464 | tf_op jit(solution)/shard_map/while/body/eval_jaxpr/ppermute | solution.py:21
  196.8 9.8 %collective-permute-start = (f32[4,1,322]{2,1,0:T(1,128)S(1)}, f32[4,1,322]{2,1,0:T(1,128)S(1)}, u32[]{:S(2)}, u32[]{:S(2)}) collective-permute-start(f32[4,1,322]{2,1,0:T(1,128)S(1)} %get-tuple-element.251), channel_id=1, source_target_pairs={{1,0},{2,1},{3,2},{4,3},{5,4},{6,5},{7,6},{9,8},{10,9},{11,10},{12... | collective-permute-start | bytes 15464 | tf_op jit(solution)/shard_map/while/body/eval_jaxpr/ppermute | solution.py:22
  198.1 9.8 %collective-permute-start.1 = (f32[4,1,322]{2,1,0:T(1,128)S(1)}, f32[4,1,322]{2,1,0:T(1,128)S(1)}, u32[]{:S(2)}, u32[]{:S(2)}) collective-permute-start(f32[4,1,322]{2,1,0:T(1,128)S(1)} %get-tuple-element.252), channel_id=1, source_target_pairs={{0,1},{1,2},{2,3},{3,4},{4,5},{5,6},{6,7},{8,9},{9,10},{10,11},{11... | collective-permute-start | bytes 15464 | tf_op jit(solution)/shard_map/while/body/eval_jaxpr/ppermute | solution.py:21
  210.1 9.8 %collective-permute-start = (f32[4,1,322]{2,1,0:T(1,128)S(1)}, f32[4,1,322]{2,1,0:T(1,128)S(1)}, u32[]{:S(2)}, u32[]{:S(2)}) collective-permute-start(f32[4,1,322]{2,1,0:T(1,128)S(1)} %get-tuple-element.251), channel_id=1, source_target_pairs={{1,0},{2,1},{3,2},{4,3},{5,4},{6,5},{7,6},{9,8},{10,9},{11,10},{12... | collective-permute-start | bytes 15464 | tf_op jit(solution)/shard_map/while/body/eval_jaxpr/ppermute | solution.py:22
  211.4 9.8 %collective-permute-start.1 = (f32[4,1,322]{2,1,0:T(1,128)S(1)}, f32[4,1,322]{2,1,0:T(1,128)S(1)}, u32[]{:S(2)}, u32[]{:S(2)}) collective-permute-start(f32[4,1,322]{2,1,0:T(1,128)S(1)} %get-tuple-element.252), channel_id=1, source_target_pairs={{0,1},{1,2},{2,3},{3,4},{4,5},{5,6},{6,7},{8,9},{9,10},{10,11},{11... | collective-permute-start | bytes 15464 | tf_op jit(solution)/shard_map/while/body/eval_jaxpr/ppermute | solution.py:21
  223.5 9.8 %collective-permute-start = (f32[4,1,322]{2,1,0:T(1,128)S(1)}, f32[4,1,322]{2,1,0:T(1,128)S(1)}, u32[]{:S(2)}, u32[]{:S(2)}) collective-permute-start(f32[4,1,322]{2,1,0:T(1,128)S(1)} %get-tuple-element.251), channel_id=1, source_target_pairs={{1,0},{2,1},{3,2},{4,3},{5,4},{6,5},{7,6},{9,8},{10,9},{11,10},{12... | collective-permute-start | bytes 15464 | tf_op jit(solution)/shard_map/while/body/eval_jaxpr/ppermute | solution.py:22
  224.8 9.8 %collective-permute-start.1 = (f32[4,1,322]{2,1,0:T(1,128)S(1)}, f32[4,1,322]{2,1,0:T(1,128)S(1)}, u32[]{:S(2)}, u32[]{:S(2)}) collective-permute-start(f32[4,1,322]{2,1,0:T(1,128)S(1)} %get-tuple-element.252), channel_id=1, source_target_pairs={{0,1},{1,2},{2,3},{3,4},{4,5},{5,6},{6,7},{8,9},{9,10},{10,11},{11... | collective-permute-start | bytes 15464 | tf_op jit(solution)/shard_map/while/body/eval_jaxpr/ppermute | solution.py:21
  236.9 9.8 %collective-permute-start = (f32[4,1,322]{2,1,0:T(1,128)S(1)}, f32[4,1,322]{2,1,0:T(1,128)S(1)}, u32[]{:S(2)}, u32[]{:S(2)}) collective-permute-start(f32[4,1,322]{2,1,0:T(1,128)S(1)} %get-tuple-element.251), channel_id=1, source_target_pairs={{1,0},{2,1},{3,2},{4,3},{5,4},{6,5},{7,6},{9,8},{10,9},{11,10},{12... | collective-permute-start | bytes 15464 | tf_op jit(solution)/shard_map/while/body/eval_jaxpr/ppermute | solution.py:22
  238.2 9.8 %collective-permute-start.1 = (f32[4,1,322]{2,1,0:T(1,128)S(1)}, f32[4,1,322]{2,1,0:T(1,128)S(1)}, u32[]{:S(2)}, u32[]{:S(2)}) collective-permute-start(f32[4,1,322]{2,1,0:T(1,128)S(1)} %get-tuple-element.252), channel_id=1, source_target_pairs={{0,1},{1,2},{2,3},{3,4},{4,5},{5,6},{6,7},{8,9},{9,10},{10,11},{11... | collective-permute-start | bytes 15464 | tf_op jit(solution)/shard_map/while/body/eval_jaxpr/ppermute | solution.py:21
  250.3 9.8 %collective-permute-start = (f32[4,1,322]{2,1,0:T(1,128)S(1)}, f32[4,1,322]{2,1,0:T(1,128)S(1)}, u32[]{:S(2)}, u32[]{:S(2)}) collective-permute-start(f32[4,1,322]{2,1,0:T(1,128)S(1)} %get-tuple-element.251), channel_id=1, source_target_pairs={{1,0},{2,1},{3,2},{4,3},{5,4},{6,5},{7,6},{9,8},{10,9},{11,10},{12... | collective-permute-start | bytes 15464 | tf_op jit(solution)/shard_map/while/body/eval_jaxpr/ppermute | solution.py:22
  251.6 9.8 %collective-permute-start.1 = (f32[4,1,322]{2,1,0:T(1,128)S(1)}, f32[4,1,322]{2,1,0:T(1,128)S(1)}, u32[]{:S(2)}, u32[]{:S(2)}) collective-permute-start(f32[4,1,322]{2,1,0:T(1,128)S(1)} %get-tuple-element.252), channel_id=1, source_target_pairs={{0,1},{1,2},{2,3},{3,4},{4,5},{5,6},{6,7},{8,9},{9,10},{10,11},{11... | collective-permute-start | bytes 15464 | tf_op jit(solution)/shard_map/while/body/eval_jaxpr/ppermute | solution.py:21
  263.7 9.8 %collective-permute-start = (f32[4,1,322]{2,1,0:T(1,128)S(1)}, f32[4,1,322]{2,1,0:T(1,128)S(1)}, u32[]{:S(2)}, u32[]{:S(2)}) collective-permute-start(f32[4,1,322]{2,1,0:T(1,128)S(1)} %get-tuple-element.251), channel_id=1, source_target_pairs={{1,0},{2,1},{3,2},{4,3},{5,4},{6,5},{7,6},{9,8},{10,9},{11,10},{12... | collective-permute-start | bytes 15464 | tf_op jit(solution)/shard_map/while/body/eval_jaxpr/ppermute | solution.py:22
  265.0 9.8 %collective-permute-start.1 = (f32[4,1,322]{2,1,0:T(1,128)S(1)}, f32[4,1,322]{2,1,0:T(1,128)S(1)}, u32[]{:S(2)}, u32[]{:S(2)}) collective-permute-start(f32[4,1,322]{2,1,0:T(1,128)S(1)} %get-tuple-element.252), channel_id=1, source_target_pairs={{0,1},{1,2},{2,3},{3,4},{4,5},{5,6},{6,7},{8,9},{9,10},{10,11},{11... | collective-permute-start | bytes 15464 | tf_op jit(solution)/shard_map/while/body/eval_jaxpr/ppermute | solution.py:21
  277.8 330.0 %copy-start.14 = (s32[128]{0:T(128)S(1)}, s32[128]{0:T(128)}, u32[]{:S(2)}) copy-start(s32[128]{0:T(128)} %and_select_fusion.5) | copy-start | bytes 1540
  277.8 330.0 %copy-start.15 = (f32[128]{0:T(128)S(1)}, f32[128]{0:T(128)}, u32[]{:S(2)}) copy-start(f32[128]{0:T(128)} %compare_convert_fusion) | copy-start | bytes 1540
  280.7 328.0 %copy-start.17 = (s32[32]{0:T(128)S(1)}, s32[32]{0:T(128)}, u32[]{:S(2)}) copy-start(s32[32]{0:T(128)} %copy-done.16) | copy-start | bytes 388
  280.7 328.0 %copy-start.19 = (pred[32]{0:T(512)(128)(4,1)S(1)}, pred[32]{0:T(512)(128)(4,1)}, u32[]{:S(2)}) copy-start(pred[32]{0:T(512)(128)(4,1)} %copy-done.18) | copy-start | bytes 100
  280.7 328.3 %copy-start.6 = (f32[4,64,129]{2,1,0:T(8,128)S(1)}, f32[4,64,129]{2,1,0:T(8,128)}, u32[]{:S(2)}) copy-start(f32[4,64,129]{2,1,0:T(8,128)} %fusion.15) | copy-start | bytes 396292
  280.7 328.3 %copy-start.8 = (f32[4,65,128]{2,1,0:T(8,128)S(1)}, f32[4,65,128]{2,1,0:T(8,128)}, u32[]{:S(2)}) copy-start(f32[4,65,128]{2,1,0:T(8,128)} %fusion.22) | copy-start | bytes 399364
  280.8 328.3 %copy-start.9 = (f32[3,64,128]{2,1,0:T(8,128)S(1)}, f32[3,64,128]{2,1,0:T(8,128)}, u32[]{:S(2)}) copy-start(f32[3,64,128]{2,1,0:T(8,128)} %fusion.30) | copy-start | bytes 294916
  280.8 328.3 %copy-start.13 = (pred[64,128]{1,0:T(8,128)(4,1)S(1)}, pred[64,128]{1,0:T(8,128)(4,1)}, u32[]{:S(2)}) copy-start(pred[64,128]{1,0:T(8,128)(4,1)} %multiply_compare_fusion) | copy-start | bytes 24580
  280.8 328.3 %copy-start.21 = (s32[128]{0:T(128)S(1)}, s32[128]{0:T(128)}, u32[]{:S(2)}) copy-start(s32[128]{0:T(128)} %copy-done.20) | copy-start | bytes 1540
  280.8 328.3 %copy-start.23 = (s32[32]{0:T(128)S(1)}, s32[32]{0:T(128)}, u32[]{:S(2)}) copy-start(s32[32]{0:T(128)} %copy-done.22) | copy-start | bytes 388
  280.8 328.3 %copy-start.25 = (pred[32]{0:T(512)(128)(4,1)S(1)}, pred[32]{0:T(512)(128)(4,1)}, u32[]{:S(2)}) copy-start(pred[32]{0:T(512)(128)(4,1)} %copy-done.24) | copy-start | bytes 100
Sparse Core Ops, SparseCore 0:
  9.7 54.6 all-gather.3
  71.8 68.9 all-gather.5
where the time goes:
time: 618 us; the launch traced here: 617 us
  blocking collectives  327 us (53%)
  waiting for transfers between devices  110 us (18%)
  starting transfers between devices  93.5 us (15%)
  other arithmetic  30.7 us (5%)
  local copies, waits for them, and re-layouts  23.2 us (4%)
  between operations  17.7 us (3%)
  matrix products  14.1 us (2%)
    all_gather x1, blocking collectives, shards(): lax.all_gather(coarse_band[None], ('grp', 'tile'), axis=0, tiled=True)  327 us
    ppermute x12, starting transfers between devices, extended(): before = lax.ppermute(last, axis, up)  78 us
    all_gather x1, waiting for transfers between devices, shards(): portion = lax.all_gather(fields, 'grp', axis=2, tiled=True)  45.3 us
    all_gather x1, waiting for transfers between devices, shards(): portion = lax.all_gather(row_window, 'tile', axis=3, tiled=True)  41 us
    ppermute x12, starting transfers between devices, extended(): after = lax.ppermute(leading, axis, down)  15.5 us
    ppermute x12, waiting for transfers between devices, extended(): before = lax.ppermute(last, axis, up)  13.2 us
  transfers between devices with their start and end apart: 26, of which 14 were waited for; matrix products, arithmetic and copies ran while one was open for 3% of the time, Pallas kernels for 0%

commit v1 on v0

v1 whole, which is shorter than its diff:
```python
import functools
import jax
import jax.numpy as jnp
from jax import lax
from jax.experimental import pallas as pl
from jax.experimental.pallas import tpu as pltpu
from jax.sharding import PartitionSpec as P

RATIO = 10
FR = 32
LEV = 4
ROWS = 64
COLS = 128
OWN = 40
WIDE = 320
GROUPS = 16
TILES = 8
SPAN = FR + 2
WIN = 40
HALO = 120
MIX = 0.02

SMEM = pl.BlockSpec(memory_space=pltpu.SMEM)
ANY = pl.BlockSpec(memory_space=pl.ANY)
VMEM = pl.BlockSpec(memory_space=pltpu.VMEM)


def width_of(chunk):
    return min(128, WIDE - 128 * chunk)


def nest_over(rows, group):
    found = jnp.int32(0)
    for i in range(GROUPS):
        found = jnp.where(rows[i] == group, jnp.int32(i), found)
    return found


def lanes(shape):
    return lax.broadcasted_iota(jnp.int32, shape, 1)


def pack_kernel(rows, offs, left, so2, east, north, diff, nest, send, edges, x, nx, win, halo, sems):
    t = lax.axis_index("tile")
    g = lax.axis_index("grp")
    loads = [
        pltpu.make_async_copy(f, x.at[pl.ds(4 * i, 4), pl.ds(0, ROWS), :], sems.at[i])
        for i, f in enumerate((so2, east, north, diff))
    ]
    loads.append(pltpu.make_async_copy(nest.at[0], nx, sems.at[4]))
    for c in loads:
        c.start()
    n = nest_over(rows, g)
    top = offs[n] - 1
    base = 128 * t + 1 - left[n] + 1024
    x[:, ROWS : ROWS + 8, :] = jnp.zeros((16, 8, 128), jnp.float32)
    lane = lanes((8, 128))
    loads[4].wait()
    for l in range(LEV):
        for m in range(3):
            w = width_of(m)
            at = 10 * (3 * l + m)
            halo[0, at : at + 10, 0:w] = nx[l, 0:10, 128 * m : 128 * m + w]
            halo[1, at : at + 10, 0:w] = nx[l, OWN - 10 : OWN, 128 * m : 128 * m + w]

    up = pltpu.make_async_copy(halo.at[0], send.at[jnp.maximum(t - 1, 0), pl.ds(WIN + 8, HALO), :], sems.at[5])
    down = pltpu.make_async_copy(
        halo.at[1], send.at[jnp.minimum(t + 1, TILES - 1), pl.ds(WIN + 8, HALO), :], sems.at[6]
    )

    @pl.when(t > 0)
    def _():
        up.start()

    @pl.when(t < TILES - 1)
    def _():
        down.start()

    for c in loads[:4]:
        c.wait()
    for l in range(LEV):
        edges[l : l + 1, :] = x[l, 0:1, :]
        edges[4 + l : 5 + l, :] = x[4 + l, 0:1, :]
        edges[8 + l : 9 + l, :] = x[l, ROWS - 1 : ROWS, :]
        edges[12 + l : 13 + l, :] = x[4 + l, ROWS - 1 : ROWS, :]
    first = jnp.zeros((8, 128), jnp.float32)
    last = jnp.zeros((8, 128), jnp.float32)
    for p in range(8):
        plane = p if p < 4 else p + 4
        for b in range(8):
            k = 8 * p + b
            v = x[plane, 8 * b : 8 * b + 8, :]
            first = jnp.where(lane == k, pltpu.roll(v, k, 1), first)
            last = jnp.where(lane == k, pltpu.roll(v, k + 1, 1), last)
    shifts = [lax.rem(base + SPAN * f, 128) for f in range(3)]
    kshifts = [lax.rem(base + 32 * l - 1, 128) for l in range(LEV)]
    for d in range(TILES):
        for l in range(LEV):
            part = [
                pltpu.roll(x[4 * f + l, pl.ds(top + 4 * d, 8), :], shifts[f], 1) for f in range(3)
            ]
            win[d, 8 * l : 8 * l + 8, :] = jnp.where(
                lane < SPAN, part[0], jnp.where(lane < 2 * SPAN, part[1], part[2])
            )
        part = [pltpu.roll(x[12 + l, pl.ds(top + 4 * d, 8), :], kshifts[l], 1) for l in range(LEV)]
        win[d, 32:40, :] = jnp.where(
            lane < 64,
            jnp.where(lane < 32, part[0], part[1]),
            jnp.where(lane < 96, part[2], part[3]),
        )
        win[d, 40:48, :] = jnp.where(d < t, first, last)
    out = pltpu.make_async_copy(win, send.at[:, pl.ds(0, WIN + 8), :], sems.at[7])
    out.start()

    @pl.when(t > 0)
    def _():
        up.wait()

    @pl.when(t < TILES - 1)
    def _():
        down.wait()

    out.wait()


def merge_kernel(rows, left, got, edges, send, a, b, sems):
    g = lax.axis_index("grp")
    n = nest_over(rows, g)
    start = left[n] - 1
    first = lax.div(start, COLS)
    second = jnp.minimum(first + 1, TILES - 1)
    load_a = pltpu.make_async_copy(got.at[first, pl.ds(0, WIN), :], a, sems.at[0])
    load_b = pltpu.make_async_copy(got.at[second, pl.ds(0, WIN), :], b, sems.at[1])
    load_a.start()
    load_b.start()
    up = pltpu.make_async_copy(
        edges.at[pl.ds(0, 8), :], send.at[jnp.maximum(g - 1, 0), pl.ds(WIN, 8), :], sems.at[2]
    )
    down = pltpu.make_async_copy(
        edges.at[pl.ds(8, 8), :], send.at[jnp.minimum(g + 1, GROUPS - 1), pl.ds(WIN, 8), :], sems.at[3]
    )

    @pl.when(g > 0)
    def _():
        up.start()

    @pl.when(g < GROUPS - 1)
    def _():
        down.start()

    room = COLS - (start - COLS * first)
    lane = lanes((32, 128))
    col = (
        lane
        - jnp.where(lane >= SPAN, SPAN, 0)
        - jnp.where(lane >= 2 * SPAN, SPAN, 0)
    )
    klane = lanes((8, 128))
    kcol = (klane & 31) + 1
    load_a.wait()
    load_b.wait()
    a[0:32, :] = jnp.where(col < room, a[0:32, :], b[0:32, :])
    a[32:40, :] = jnp.where(kcol < room, a[32:40, :], b[32:40, :])
    out = pltpu.make_async_copy(a, send.at[n, pl.ds(0, WIN), :], sems.at[4])
    out.start()

    @pl.when(g > 0)
    def _():
        up.wait()

    @pl.when(g < GROUPS - 1)
    def _():
        down.wait()

    out.wait()


def from_left(chunks, lane):
    turned = [pltpu.roll(c, 1, 1) for c in chunks]
    return [jnp.where(lane == 0, turned[m - 1], turned[m]) for m in range(3)]


def from_right(chunks, lane):
    turned = [pltpu.roll(c, 127, 1) for c in chunks]
    return [jnp.where(lane == 127, turned[(m + 1) % 3], turned[m]) for m in range(3)]


def pos(v):
    return jnp.maximum(v, 0.0)


def neg(v):
    return jnp.minimum(v, 0.0)


def fine_kernel(
    rows, left, height, width, got_tile, got_grp, nest, so2, east, north, diff,
    fine_out, back, stepped,
    w, hn, nx, eh, ch, px, vk, e, c, u, v, kz, raw, am, ap, bm, bp, ac, sums, slot, sems,
):
    t = lax.axis_index("tile")
    g = lax.axis_index("grp")
    src = rows[g]
    prev_t = jnp.maximum(t - 1, 0)
    next_t = jnp.minimum(t + 1, TILES - 1)
    prev_g = jnp.maximum(g - 1, 0)
    next_g = jnp.minimum(g + 1, GROUPS - 1)
    copies = [
        (got_grp.at[src, pl.ds(0, WIN), :], w),
        (nest.at[0], nx),
        (got_tile.at[prev_t, pl.ds(WIN + 8, HALO), :], hn.at[0]),
        (got_tile.at[next_t, pl.ds(WIN + 8, HALO), :], hn.at[1]),
        (so2, px.at[pl.ds(0, 4), pl.ds(8, ROWS), :]),
        (east, px.at[pl.ds(4, 4), pl.ds(8, ROWS), :]),
        (north, vk.at[pl.ds(0, 4)]),
        (diff, vk.at[pl.ds(4, 4)]),
        (got_grp.at[prev_g, pl.ds(WIN, 8), :], eh.at[0]),
        (got_grp.at[next_g, pl.ds(WIN, 8), :], eh.at[1]),
        (got_tile.at[prev_t, pl.ds(WIN, 8), :], ch.at[0]),
        (got_tile.at[next_t, pl.ds(WIN, 8), :], ch.at[1]),
    ]
    copies = [pltpu.make_async_copy(s, d, sems.at[i]) for i, (s, d) in enumerate(copies)]
    for copy in copies:
        copy.start()
    lane = lanes((8, 128))
    sub = lax.broadcasted_iota(jnp.int32, (8, 128), 0)
    zero = jnp.zeros((8, 128), jnp.float32)
    for p in range(2):
        for l in range(LEV):
            for m in range(3):
                c[p, l, m, 0:8, :] = zero
                c[p, l, m, 72:80, :] = zero
    copies[0].wait()
    for m in range(3):
        fine_col = 128 * m + lane
        under = (fine_col * 6554) >> 16
        pick = jnp.where(fine_col < WIDE, under + 1, jnp.where(fine_col == WIDE, SPAN - 1, 0))
        kpick = jnp.minimum(under, FR - 1)
        for l in range(LEV):
            block = w[8 * l : 8 * l + 8, :]
            for f in range(3):
                e[4 * f + l, m] = jnp.take_along_axis(block, pick + SPAN * f, axis=1)
            e[12 + l, m] = jnp.take_along_axis(w[32:40, :], kpick + 32 * l, axis=1)
    copies[1].wait()
    copies[2].wait()
    copies[3].wait()
    for l in range(LEV):
        for m in range(3):
            n = width_of(m)
            at = 10 * (3 * l + m)
            raw[l, m, 8:18, :] = hn[0, at : at + 10, :]
            raw[l, m, 18:58, 0:n] = nx[l, :, 128 * m : 128 * m + n]
            raw[l, m, 58:68, :] = hn[1, at : at + 10, :]
    last_row = RATIO * height[g]
    last_col = RATIO * width[g]
    first_row = OWN * t - 10

    def spread(p, m, i):
        lo, hi = (8 * i) // 10, min((8 * i + 7) // 10, 5)
        low = jnp.broadcast_to(e[p, m, lo : lo + 1, :], (8, 128))
        if lo == hi:
            return low
        high = jnp.broadcast_to(e[p, m, hi : hi + 1, :], (8, 128))
        return jnp.where(sub < 10 * hi - 8 * i, low, high)

    for i in range(8):
        r = 8 + 8 * i
        row = first_row + 8 * i + sub
        row_in = (row >= 0) & (row < last_row)
        for m in range(3):
            active = row_in & (128 * m + lane < last_col)
            for l in range(LEV):
                c[0, l, m, r : r + 8, :] = jnp.where(active, raw[l, m, r : r + 8, :], spread(l, m, i))
                u[l, m, r : r + 8, :] = spread(4 + l, m, i)
                v[l, m, r : r + 8, :] = spread(8 + l, m, i)
    for i in range(8):
        r = 8 + 8 * i
        local = 8 * i + sub
        row = first_row + local
        row_in = (row >= 0) & (row < last_row) & (local >= 1) & (local <= 58)
        inside = [row_in & (128 * m + lane < last_col) for m in range(3)]
        faces = []
        for m in range(3):
            ks = [spread(12 + l, m, i) for l in range(LEV)]
            faces.append([(0.05 * (ks[l] + ks[l + 1])) for l in range(LEV - 1)])
            for l in range(LEV - 1):
                kz[l, m, 8 * i : 8 * i + 8, :] = jnp.where(inside[m], faces[m][l], 0.0)
        for l in range(LEV):
            vs = [v[l, m, r : r + 8, :] for m in range(3)]
            before = from_left(vs, lane)
            after = from_right(vs, lane)
            for m in range(3):
                here = u[l, m, r : r + 8, :]
                u_lo = 0.5 * (u[l, m, r - 1 : r + 7, :] + here)
                u_hi = 0.5 * (here + u[l, m, r + 1 : r + 9, :])
                v_lo = 0.5 * (before[m] + vs[m])
                v_hi = 0.5 * (vs[m] + after[m])
                mid = (1.0 - 4.0 * MIX) - pos(u_hi) + neg(u_lo) - pos(v_hi) + neg(v_lo)
                if l > 0:
                    mid = mid - faces[m][l - 1]
                if l < LEV - 1:
                    mid = mid - faces[m][l]
                q = slice(8 * i, 8 * i + 8)
                ac[l, m, q, :] = jnp.where(inside[m], mid, 1.0)
                am[l, m, q, :] = jnp.where(inside[m], MIX + pos(u_lo), 0.0)
                ap[l, m, q, :] = jnp.where(inside[m], MIX - neg(u_hi), 0.0)
                bm[l, m, q, :] = jnp.where(inside[m], MIX + pos(v_lo), 0.0)
                bp[l, m, q, :] = jnp.where(inside[m], MIX - neg(v_hi), 0.0)

    def advance(old, new):
        for i in range(8):
            r = 8 + 8 * i
            q = slice(8 * i, 8 * i + 8)
            now = [[c[old, l, m, r : r + 8, :] for m in range(3)] for l in range(LEV)]
            flow = [[kz[l, m, q, :] for m in range(3)] for l in range(LEV - 1)]
            for l in range(LEV):
                before = from_left(now[l], lane)
                after = from_right(now[l], lane)
                for m in range(3):
                    value = ac[l, m, q, :] * now[l][m]
                    value = value + am[l, m, q, :] * c[old, l, m, r - 1 : r + 7, :]
                    value = value + ap[l, m, q, :] * c[old, l, m, r + 1 : r + 9, :]
                    value = value + bm[l, m, q, :] * before[m]
                    value = value + bp[l, m, q, :] * after[m]
                    if l > 0:
                        value = value + flow[l - 1][m] * now[l - 1][m]
                    if l < LEV - 1:
                        value = value + flow[l][m] * now[l + 1][m]
                    c[new, l, m, r : r + 8, :] = value

    def pair(_, carry):
        advance(0, 1)
        advance(1, 0)
        return carry

    lax.fori_loop(0, RATIO // 2, pair, 0)
    for l in range(LEV):
        for m in range(3):
            n = width_of(m)
            fine_out[0, l, :, 128 * m : 128 * m + n] = c[0, l, m, 18:58, 0:n]
            for a in range(4):
                band = c[0, l, m, 18 + 10 * a : 28 + 10 * a, :]
                sums[m, 4 * l + a : 4 * l + a + 1, :] = jnp.sum(band, axis=0, keepdims=True)
    mean = jnp.zeros((16, 128), jnp.float32)
    for m in range(3):
        k = 128 * m + lax.broadcasted_iota(jnp.int32, (128, 128), 0)
        chosen = ((k * 6554) >> 16) == lanes((128, 128))
        pick = jnp.where(chosen & (k < WIDE), 1.0, 0.0)
        mean = mean + jnp.dot(
            sums[m], pick, precision=lax.Precision.HIGHEST, preferred_element_type=jnp.float32
        )
    mean = mean * (1.0 / (RATIO * RATIO))
    lane4 = lanes((4, 128))
    value = jnp.zeros((4, 128), jnp.float32)
    turned = [mean if l == 0 else pltpu.roll(mean, 32 * l, 1) for l in range(LEV)]
    for l in range(LEV):
        inside = (lane4 >= 32 * l) & (lane4 < 32 * l + 32)
        value = jnp.where(inside, turned[l][4 * l : 4 * l + 4, :], value)
    slot[...] = value
    tile_a = lax.div(left[g], COLS)
    tile_b = jnp.where(tile_a < TILES - 1, tile_a + 1, tile_a - 1)
    send_a = pltpu.make_async_copy(slot, back.at[TILES * src + tile_a], sems.at[12])
    send_b = pltpu.make_async_copy(slot, back.at[TILES * src + tile_b], sems.at[13])
    send_a.start()
    send_b.start()

    for copy in copies[4:]:
        copy.wait()
    for p in range(8):
        px[p, 7:8, :] = jnp.where(g > 0, eh[0, p : p + 1, :], 0.0)
        px[p, 72:73, :] = jnp.where(g < GROUPS - 1, eh[1, p : p + 1, :], 0.0)
    edge_l = jnp.where(t > 0, ch[0], 0.0)
    edge_r = jnp.where(t < TILES - 1, ch[1], 0.0)
    for b in range(8):
        r = 8 + 8 * b
        q = slice(8 * b, 8 * b + 8)
        now = [px[l, r : r + 8, :] for l in range(LEV)]
        ks = [vk[4 + l, q, :] for l in range(LEV)]
        between = [0.5 * (ks[l] + ks[l + 1]) * (now[l + 1] - now[l]) for l in range(LEV - 1)]
        for l in range(LEV):
            here = now[l]
            k, kv = 8 * l + b, 32 + 8 * l + b
            wind = vk[l, q, :]
            c_w = jnp.where(lane == 0, pltpu.roll(edge_l, (128 - k) % 128, 1), pltpu.roll(here, 1, 1))
            c_e = jnp.where(lane == 127, pltpu.roll(edge_r, 127 - k, 1), pltpu.roll(here, 127, 1))
            v_w = jnp.where(lane == 0, pltpu.roll(edge_l, 128 - kv, 1), pltpu.roll(wind, 1, 1))
            v_e = jnp.where(lane == 127, pltpu.roll(edge_r, 127 - kv, 1), pltpu.roll(wind, 127, 1))
            c_n = px[l, r - 1 : r + 7, :]
            c_s = px[l, r + 1 : r + 9, :]
            flow = px[4 + l, r : r + 8, :]
            u_lo = 0.5 * (px[4 + l, r - 1 : r + 7, :] + flow)
            u_hi = 0.5 * (flow + px[4 + l, r + 1 : r + 9, :])
            v_lo = 0.5 * (v_w + wind)
            v_hi = 0.5 * (wind + v_e)
            value = (
                here
                - ((pos(u_hi) * here + neg(u_hi) * c_s) - (pos(u_lo) * c_n + neg(u_lo) * here))
                - ((pos(v_hi) * here + neg(v_hi) * c_e) - (pos(v_lo) * c_w + neg(v_lo) * here))
                + MIX * (c_n + c_s + c_w + c_e - 4.0 * here)
            )
            if l < LEV - 1:
                value = value + between[l]
            if l > 0:
                value = value - between[l - 1]
            stepped[l, q, :] = value
    send_a.wait()
    send_b.wait()


def place_kernel(rows, offs, left, height, width, stepped, got, out, s, r, sems):
    t = lax.axis_index("tile")
    g = lax.axis_index("grp")
    n = nest_over(rows, g)
    lf = left[n]
    wd = width[n]

    @pl.when((lf < COLS * t + COLS) & (lf + wd > COLS * t))
    def _():
        off = offs[n]
        base = pl.multiple_of(lax.div(off, 8) * 8, 8)
        load_s = pltpu.make_async_copy(stepped.at[:, pl.ds(base, 40), :], s, sems.at[0])
        load_r = pltpu.make_async_copy(got.at[n], r, sems.at[1])
        load_s.start()
        load_r.start()
        lane = lanes((FR, 128)) + COLS * t
        row = lax.broadcasted_iota(jnp.int32, (FR, 128), 0)
        covered = (lane >= lf) & (lane < lf + wd) & (row < height[n])
        load_s.wait()
        load_r.wait()
        for l in range(LEV):
            turned = pltpu.roll(r[...], lax.rem(lf - COLS * t - 32 * l + 2048, 128), 1)
            at = pl.ds(off - base, FR)
            s[l, at, :] = jnp.where(covered, turned, s[l, at, :])
        store = pltpu.make_async_copy(s, out.at[:, pl.ds(base, 40), :], sems.at[2])
        store.start()
        store.wait()


def shards(so2, east, north, diff, nest, rows, offs, left, height, width):
    f32 = jnp.float32
    shape = jax.ShapeDtypeStruct
    dma = pltpu.SemaphoreType.DMA
    send, edges = pl.pallas_call(
        pack_kernel,
        out_shape=(shape((TILES, WIN + 8 + HALO, 128), f32), shape((16, 128), f32)),
        in_specs=[SMEM] * 3 + [ANY] * 5,
        out_specs=(ANY, VMEM),
        scratch_shapes=[
            pltpu.VMEM((16, ROWS + 8, 128), f32),
            pltpu.VMEM((LEV, OWN, WIDE), f32),
            pltpu.VMEM((TILES, WIN + 8, 128), f32),
            pltpu.VMEM((2, HALO, 128), f32),
            dma((8,)),
        ],
        name="pack",
    )(rows, offs, left, so2, east, north, diff, nest)
    got_tile = lax.all_to_all(send, "tile", 0, 0)
    send = pl.pallas_call(
        merge_kernel,
        out_shape=shape((GROUPS, WIN + 8, 128), f32),
        in_specs=[SMEM] * 2 + [ANY, VMEM],
        out_specs=ANY,
        scratch_shapes=[pltpu.VMEM((WIN, 128), f32), pltpu.VMEM((WIN, 128), f32), dma((5,))],
        name="merge",
    )(rows, left, got_tile, edges)
    got_grp = lax.all_to_all(send, "grp", 0, 0)
    field = functools.partial(pltpu.VMEM, dtype=f32)
    nest_next, back, stepped = pl.pallas_call(
        fine_kernel,
        out_shape=(
            shape((1, LEV, OWN, WIDE), f32),
            shape((GROUPS * TILES, 4, 128), f32),
            shape((LEV, ROWS, COLS), f32),
        ),
        in_specs=[SMEM] * 4 + [ANY] * 7,
        out_specs=(VMEM, ANY, VMEM),
        scratch_shapes=[
            field((WIN, 128)),
            field((2, HALO, 128)),
            field((LEV, OWN, WIDE)),
            field((2, 8, 128)),
            field((2, 8, 128)),
            field((8, ROWS + 16, 128)),
            field((8, ROWS, 128)),
            field((16, 3, 8, 128)),
            field((2, LEV, 3, 80, 128)),
            field((LEV, 3, 80, 128)),
            field((LEV, 3, 80, 128)),
            field((LEV - 1, 3, 64, 128)),
            field((LEV, 3, 80, 128)),
            field((LEV, 3, 64, 128)),
            field((LEV, 3, 64, 128)),
            field((LEV, 3, 64, 128)),
            field((LEV, 3, 64, 128)),
            field((LEV, 3, 64, 128)),
            field((3, 16, 128)),
            field((4, 128)),
            dma((14,)),
        ],
        name="fine",
    )(rows, left, height, width, got_tile, got_grp, nest, so2, east, north, diff)
    got = lax.all_to_all(back, ("grp", "tile"), 0, 0)
    got = got.reshape(GROUPS, FR, 128)
    parent_next = pl.pallas_call(
        place_kernel,
        out_shape=shape((LEV, ROWS, COLS), f32),
        in_specs=[SMEM] * 5 + [ANY, ANY],
        out_specs=ANY,
        scratch_shapes=[field((LEV, 40, 128)), field((FR, 128)), dma((3,))],
        input_output_aliases={5: 0},
        name="place",
    )(rows, offs, left, height, width, stepped, got)
    return parent_next, nest_next


def solution(mesh):
    in_specs = (
        P(None, "grp", "tile"),
        P(None, "grp", "tile"),
        P(None, "grp", "tile"),
        P(None, "grp", "tile"),
        P("grp", None, "tile", None),
        P(),
        P(),
        P(),
        P(),
        P(),
    )
    out_specs = (P(None, "grp", "tile"), P("grp", None, "tile", None))
    return jax.shard_map(shards, mesh=mesh, in_specs=in_specs, out_specs=out_specs, check_vma=False)
```

time: 618 us -> 68 us (0.11)
  the two profiles are of different devices: /device:TPU:0 before, /device:TPU:1 now
where the time goes in v1:
time: 68 us; the launch traced here: 67 us
  blocking collectives  52.6 us (77%)
  Pallas kernels  13.7 us (20%)
    all_to_all x1, blocking collectives, shards(): got_tile = lax.all_to_all(send, 'tile', 0, 0)  21 us
    all_to_all x1, blocking collectives, shards(): got = lax.all_to_all(back, ('grp', 'tile'), 0, 0)  16.4 us
    all_to_all x1, blocking collectives, shards(): got_grp = lax.all_to_all(send, 'grp', 0, 0)  15.2 us
    pallas_call x1, Pallas kernels, shards(): pl.pallas_call(fine_kernel, out_shape=(shape((1, LEV, OWN, WIDE), f32), s...  7.24 us
    pallas_call x1, Pallas kernels, shards(): pl.pallas_call(pack_kernel, out_shape=(shape((TILES, WIN + 8 + HALO, 128)...  3.6 us
    pallas_call x1, Pallas kernels, shards(): pl.pallas_call(merge_kernel, out_shape=shape((GROUPS, WIN + 8, 128), f32)...  2.12 us

profile of v1, /device:TPU:1, one launch (start us, length us, event | category | flops | bytes accessed | tf_op | source)
XLA Modules:
  0.0 67.0 jit_solution(17716097465576891421)
XLA Ops:
  0.6 3.6 %pack.1 = (f32[8,168,128]{2,1,0:T(8,128)}, f32[16,128]{1,0:T(8,128)}) custom-call(s32[16]{0:T(128)} %rows.7, s32[16]{0:T(128)} %offs.3, s32[16]{0:T(128)} %left.7, f32[4,64,128]{2,1,0:T(8,128)} %so2.3, f32[4,64,128]{2,1,0:T(8,128)} %east.3, f32[4,64,128]{2,1,0:T(8,128)} %north.3, f32[4,64,128]{2,1,0:T(8,128)} %diff.3, f32[1,4,40,320]{3,2,1,0:T(8,128)} %nest.3), custom_call_target="tpu_custom_call" | custom-call | tf_op jit(solution)/shard_map/pack/pallas_call | solution.py:443
  4.2 21.0 %all_to_all.15.got.got_tile = f32[8,168,128]{2,1,0:T(8,128)} all-to-all(f32[8,168,128]{2,1,0:T(8,128)} %get-tuple-element.7), channel_id=1, replica_groups=mesh['grp'=16,'tile'=8] {'tile'}, dimensions={0} | all-to-all | bytes 1376256 | tf_op jit(solution)/shard_map/all_to_all | solution.py:457
  25.2 2.1 %merge.1 = f32[16,48,128]{2,1,0:T(8,128)} custom-call(s32[16]{0:T(128)} %rows.7, s32[16]{0:T(128)} %left.7, f32[8,168,128]{2,1,0:T(8,128)} %all_to_all.15.got.got_tile, f32[16,128]{1,0:T(8,128)} %get-tuple-element.8.edges), custom_call_target="tpu_custom_call" | custom-call | tf_op jit(solution)/shard_map/merge/pallas_call | solution.py:458
  27.3 15.2 %all_to_all.16.got_grp = f32[16,48,128]{2,1,0:T(8,128)} all-to-all(f32[16,48,128]{2,1,0:T(8,128)} %merge.1), channel_id=1, replica_groups=mesh['grp'=16,'tile'=8] {'grp'}, dimensions={0} | all-to-all | bytes 786432 | tf_op jit(solution)/shard_map/all_to_all | solution.py:466
  42.6 7.2 %fine.1 = (f32[1,4,40,320]{3,2,1,0:T(8,128)}, f32[128,4,128]{2,1,0:T(4,128)}, f32[4,64,128]{2,1,0:T(8,128)}) custom-call(s32[16]{0:T(128)} %rows.7, s32[16]{0:T(128)} %left.7, s32[16]{0:T(128)} %height.3, s32[16]{0:T(128)} %width.3, f32[8,168,128]{2,1,0:T(8,128)} %all_to_all.15.got.got_tile, f32[16,48,128]{2,1,0:T(8,128)} %all_to_all.16.got_grp, ...), custom_call_target="tpu_custom_call" | custom-call | tf_op jit(solution)/shard_map/fine/pallas_call | solution.py:468
  49.8 16.4 %all_to_all.17 = f32[128,4,128]{2,1,0:T(4,128)} all-to-all(f32[128,4,128]{2,1,0:T(4,128)} %get-tuple-element.10), channel_id=1, replica_groups=mesh['grp'=16,'tile'=8] {'grp','tile'}, dimensions={0} | all-to-all | bytes 524288 | tf_op jit(solution)/shard_map/all_to_all | solution.py:502
  66.2 0.8 %place.1 = f32[4,64,128]{2,1,0:T(8,128)} custom-call(s32[16]{0:T(128)} %rows.7, s32[16]{0:T(128)} %offs.3, s32[16]{0:T(128)} %left.7, s32[16]{0:T(128)} %height.3, s32[16]{0:T(128)} %width.3, f32[4,64,128]{2,1,0:T(8,128)} %get-tuple-element.9.stepped, f32[16,32,128]{2,1,0:T(8,128)} %bitcast.1), custom_call_target="tpu_custom_call", output_to_operand_aliasing={{}: (5, {})} | custom-call | tf_op jit(solution)/shard_map/place/pallas_call | solution.py:504
